TPU v7x, 512 devices: a whole 4x8x8 slice. The times are simulated.
512 devices in a mesh: row: 32 (over x, y), col: 16 (over z, core).
Axes of the slice: x: 4, y: 8, z: 8, core: 2. Of those that a mesh axis runs over, the one named last changes fastest.
Arguments:
- panel_block: float32 [32768, 256], P('row', 'col'), as said below
- trailing: float32 [32768, 8192], P('row', 'col'), may hold values from -6 to 6
Outputs:
- r_factor: float32 [256, 256], replicated
- coupling: float32 [256, 8192], P(None, 'col')
- updated: float32 [32768, 8192], P('row', 'col')
Inputs may be any that keep to these rules, and one draw needn't show every extreme that they name: `panel_block`: every device's 1024 rows of the panel have full column rank and are well conditioned on their own.
All inputs are finite; a program needn't handle non-finite values.
Results may differ from a plain program's by a relative error of at most 0.00012.
Values sent between devices are 32-bit elements; how exact they have to be, the bound alone decides.
A program may use at most 64 MiB of HBM per device.

v0:
```python
import jax
import jax.numpy as jnp
from jax import lax
from jax.sharding import PartitionSpec as P

HIGHEST_PRECISION = lax.Precision.HIGHEST


def passed_along(block, axis, distance):
    devices = range(lax.axis_size(axis))
    route = [((i - distance) % len(devices), i) for i in devices]
    return lax.ppermute(block, axis, route)


def inner_gram(left_mat, right_mat):
    return lax.dot_general(
        left_mat,
        right_mat,
        (((0,), (0,)), ((), ())),
        precision=HIGHEST_PRECISION,
        preferred_element_type=jnp.float32,
    )


def solve_lower(lower_mat, matrix):
    return jax.scipy.linalg.solve_triangular(lower_mat, matrix.T, lower=True).T


def factor_pass(matrix):
    gram_mat = inner_gram(matrix, matrix)
    chol_lower = jnp.linalg.cholesky(gram_mat)
    return (solve_lower(chol_lower, matrix), chol_lower.T)


def two_pass(matrix):
    first_q, first_r = factor_pass(matrix)
    second_q, second_r = factor_pass(first_q)
    return (second_q, jnp.dot(second_r, first_r, precision=HIGHEST_PRECISION))


def stacked_factor(top_part, bottom_part):
    joined_gram = inner_gram(top_part, top_part) + inner_gram(bottom_part, bottom_part)
    return jnp.linalg.cholesky(joined_gram).T


def shards(panel_block, trailing):
    full_panel = lax.all_gather(panel_block, "col", axis=1, tiled=True)
    tree_depth = lax.axis_size("row").bit_length() - 1
    running = two_pass(full_panel)[1]
    for tree_level in range(tree_depth):
        received = passed_along(running, "row", -(1 << tree_level))
        running = stacked_factor(running, received)
    q_local = solve_lower(running.T, full_panel)
    coupling = lax.psum(inner_gram(q_local, trailing), "row")
    updated = trailing - jnp.dot(q_local, coupling, precision=HIGHEST_PRECISION)
    return (running, coupling, updated)


def solution(mesh):
    in_specs = (P("row", "col"), P("row", "col"))
    out_specs = (P(), P(None, "col"), P("row", "col"))
    return jax.shard_map(shards, mesh=mesh, in_specs=in_specs, out_specs=out_specs, check_vma=False)
```

profile of v0, /device:TPU:64, one launch (start us, length us, event | category | flops | bytes accessed | tf_op | source)
XLA Modules:
  0.0 614.6 jit_solution(14918157190939473008)
XLA Ops:
  8.0 47.0 %all-gather.2.cloned.1.call-done = f32[1024,256]{0,1:T(8,128)} async-done(((f32[1024,16]{0,1:T(8,128)}), f32[1024,256]{0,1:T(8,128)}) %all-gather.2.cloned.1.call-update) | async-done | bytes 1048592 | tf_op jit(solution)/shard_map/all_gather | solution.py:47
  54.9 2.6 fusion.121
  57.7 11.7 %cholesky.340 = f32[128,128]{1,0:T(8,128)S(1)} custom-call(f32[128,128]{1,0:T(8,128)S(1)} %cholesky.574), custom_call_target="Cholesky" | custom-call | tf_op jit(solution)/shard_map/jit(cholesky)/cholesky | solution.py:31
  69.5 9.8 %custom-call.18 = f32[1,128,128]{1,2,0:T(8,128)S(1)} custom-call(f32[1,128,128]{2,1,0:T(8,128)S(1)} %get-tuple-element.73), custom_call_target="InvertDiagBlocksLowerTriangular" | custom-call | tf_op jit(solution)/shard_map/jit(cholesky)/cholesky | solution.py:31
  79.8 11.7 %cholesky.357 = f32[128,128]{1,0:T(8,128)S(1)} custom-call(f32[128,128]{1,0:T(8,128)S(1)} %convolution_subtract_fusion.4), custom_call_target="Cholesky" | custom-call | tf_op jit(solution)/shard_map/jit(cholesky)/cholesky | solution.py:31
  93.7 4.1 while.4
  94.4 1.4 bitcast_dynamic-update-slice_fusion.4
  96.4 1.4 bitcast_dynamic-update-slice_fusion.4
  97.8 20.0 %custom-call.19 = f32[2,128,128]{1,2,0:T(8,128)S(1)} custom-call(f32[2,128,128]{2,1,0:T(8,128)S(1)} %get-tuple-element.19), custom_call_target="InvertDiagBlocksLowerTriangular" | custom-call | tf_op jit(solution)/shard_map/jit(_solve_triangular)/triangular_solve | solution.py:26
  119.8 1.0 fusion
  121.0 11.7 %cholesky.374 = f32[128,128]{1,0:T(8,128)S(1)} custom-call(f32[128,128]{1,0:T(8,128)S(1)} %cholesky.577), custom_call_target="Cholesky" | custom-call | tf_op jit(solution)/shard_map/jit(cholesky)/cholesky | solution.py:31
  133.4 9.8 %custom-call.20 = f32[1,128,128]{1,2,0:T(8,128)S(1)} custom-call(f32[1,128,128]{2,1,0:T(8,128)S(1)} %get-tuple-element.69), custom_call_target="InvertDiagBlocksLowerTriangular" | custom-call | tf_op jit(solution)/shard_map/jit(cholesky)/cholesky | solution.py:31
  143.7 11.9 %cholesky.391 = f32[128,128]{1,0:T(8,128)S(1)} custom-call(f32[128,128]{1,0:T(8,128)S(1)} %convolution_subtract_fusion.3), custom_call_target="Cholesky" | custom-call | tf_op jit(solution)/shard_map/jit(cholesky)/cholesky | solution.py:31
  158.1 6.9 %collective-permute-start = (f32[256,256]{1,0:T(8,128)S(1)}, f32[256,256]{1,0:T(8,128)S(1)}, u32[]{:S(2)}, u32[]{:S(2)}) collective-permute-start(f32[256,256]{1,0:T(8,128)S(1)} %fusion.24), channel_id=1, source_target_pairs={{16,0},{32,16},{48,32},{64,48},{80,64},{96,80},{112,96},{128,112},... | collective-permute-start | bytes 786440 | tf_op jit(solution)/shard_map/ppermute | solution.py:12
  165.5 5.3 collective-permute-done
  171.7 11.7 %cholesky.408 = f32[128,128]{1,0:T(8,128)S(1)} custom-call(f32[128,128]{1,0:T(8,128)S(1)} %cholesky.580), custom_call_target="Cholesky" | custom-call | tf_op jit(solution)/shard_map/jit(cholesky)/cholesky | solution.py:43
  184.0 9.8 %custom-call.21 = f32[1,128,128]{1,2,0:T(8,128)S(1)} custom-call(f32[1,128,128]{2,1,0:T(8,128)S(1)} %get-tuple-element.65), custom_call_target="InvertDiagBlocksLowerTriangular" | custom-call | tf_op jit(solution)/shard_map/jit(cholesky)/cholesky | solution.py:43
  194.4 11.7 %cholesky.425 = f32[128,128]{1,0:T(8,128)S(1)} custom-call(f32[128,128]{1,0:T(8,128)S(1)} %slice_subtract_fusion.4), custom_call_target="Cholesky" | custom-call | tf_op jit(solution)/shard_map/jit(cholesky)/cholesky | solution.py:43
  208.1 5.5 collective-permute-start.1
  214.0 8.5 %collective-permute-done.1 = f32[256,256]{0,1:T(8,128)S(1)} collective-permute-done((f32[256,256]{0,1:T(8,128)S(1)}, f32[256,256]{0,1:T(8,128)S(1)}, u32[]{:S(2)}, u32[]{:S(2)}) %collective-permute-start.1) | collective-permute-done | bytes 262176 | tf_op jit(solution)/shard_map/ppermute | solution.py:12
  223.1 11.7 %cholesky.442 = f32[128,128]{1,0:T(8,128)S(1)} custom-call(f32[128,128]{1,0:T(8,128)S(1)} %cholesky.583), custom_call_target="Cholesky" | custom-call | tf_op jit(solution)/shard_map/jit(cholesky)/cholesky | solution.py:43
  235.5 9.8 %custom-call.22 = f32[1,128,128]{1,2,0:T(8,128)S(1)} custom-call(f32[1,128,128]{2,1,0:T(8,128)S(1)} %get-tuple-element.61), custom_call_target="InvertDiagBlocksLowerTriangular" | custom-call | tf_op jit(solution)/shard_map/jit(cholesky)/cholesky | solution.py:43
  245.8 11.7 %cholesky.459 = f32[128,128]{1,0:T(8,128)S(1)} custom-call(f32[128,128]{1,0:T(8,128)S(1)} %slice_subtract_fusion.3), custom_call_target="Cholesky" | custom-call | tf_op jit(solution)/shard_map/jit(cholesky)/cholesky | solution.py:43
  259.6 3.7 collective-permute-start.2
  263.7 10.8 %collective-permute-done.2 = f32[256,256]{0,1:T(8,128)S(1)} collective-permute-done((f32[256,256]{0,1:T(8,128)S(1)}, f32[256,256]{0,1:T(8,128)S(1)}, u32[]{:S(2)}, u32[]{:S(2)}) %collective-permute-start.2) | collective-permute-done | bytes 262176 | tf_op jit(solution)/shard_map/ppermute | solution.py:12
  275.1 11.7 %cholesky.476 = f32[128,128]{1,0:T(8,128)S(1)} custom-call(f32[128,128]{1,0:T(8,128)S(1)} %cholesky.586), custom_call_target="Cholesky" | custom-call | tf_op jit(solution)/shard_map/jit(cholesky)/cholesky | solution.py:43
  287.5 9.8 %custom-call.23 = f32[1,128,128]{1,2,0:T(8,128)S(1)} custom-call(f32[1,128,128]{2,1,0:T(8,128)S(1)} %get-tuple-element.57), custom_call_target="InvertDiagBlocksLowerTriangular" | custom-call | tf_op jit(solution)/shard_map/jit(cholesky)/cholesky | solution.py:43
  297.8 11.7 %cholesky.493 = f32[128,128]{1,0:T(8,128)S(1)} custom-call(f32[128,128]{1,0:T(8,128)S(1)} %slice_subtract_fusion.2), custom_call_target="Cholesky" | custom-call | tf_op jit(solution)/shard_map/jit(cholesky)/cholesky | solution.py:43
  311.6 4.4 collective-permute-start.3
  316.4 5.3 collective-permute-done.3
  322.4 11.7 %cholesky.510 = f32[128,128]{1,0:T(8,128)S(1)} custom-call(f32[128,128]{1,0:T(8,128)S(1)} %cholesky.589), custom_call_target="Cholesky" | custom-call | tf_op jit(solution)/shard_map/jit(cholesky)/cholesky | solution.py:43
  334.8 9.8 %custom-call.24 = f32[1,128,128]{1,2,0:T(8,128)S(1)} custom-call(f32[1,128,128]{2,1,0:T(8,128)S(1)} %get-tuple-element.53), custom_call_target="InvertDiagBlocksLowerTriangular" | custom-call | tf_op jit(solution)/shard_map/jit(cholesky)/cholesky | solution.py:43
  345.1 11.7 %cholesky.527 = f32[128,128]{1,0:T(8,128)S(1)} custom-call(f32[128,128]{1,0:T(8,128)S(1)} %slice_subtract_fusion.1), custom_call_target="Cholesky" | custom-call | tf_op jit(solution)/shard_map/jit(cholesky)/cholesky | solution.py:43
  358.8 3.4 collective-permute-start.4
  362.7 6.2 %collective-permute-done.4 = f32[256,256]{0,1:T(8,128)S(1)} collective-permute-done((f32[256,256]{0,1:T(8,128)S(1)}, f32[256,256]{0,1:T(8,128)S(1)}, u32[]{:S(2)}, u32[]{:S(2)}) %collective-permute-start.4) | collective-permute-done | bytes 262176 | tf_op jit(solution)/shard_map/ppermute | solution.py:12
  369.5 11.7 %cholesky.544 = f32[128,128]{1,0:T(8,128)S(1)} custom-call(f32[128,128]{1,0:T(8,128)S(1)} %cholesky.592), custom_call_target="Cholesky" | custom-call | tf_op jit(solution)/shard_map/jit(cholesky)/cholesky | solution.py:43
  381.9 9.8 %custom-call.25 = f32[1,128,128]{1,2,0:T(8,128)S(1)} custom-call(f32[1,128,128]{2,1,0:T(8,128)S(1)} %get-tuple-element.49), custom_call_target="InvertDiagBlocksLowerTriangular" | custom-call | tf_op jit(solution)/shard_map/jit(cholesky)/cholesky | solution.py:43
  392.2 11.7 %cholesky.561 = f32[128,128]{1,0:T(8,128)S(1)} custom-call(f32[128,128]{1,0:T(8,128)S(1)} %slice_subtract_fusion), custom_call_target="Cholesky" | custom-call | tf_op jit(solution)/shard_map/jit(cholesky)/cholesky | solution.py:43
  405.9 0.7 fusion.16
  407.3 5.5 while.5
  408.2 2.0 bitcast_dynamic-update-slice_fusion.5
  410.8 2.0 bitcast_dynamic-update-slice_fusion.5
  412.8 20.6 %custom-call.26 = f32[2,128,128]{1,2,0:T(8,128)S(1)} custom-call(f32[2,128,128]{2,1,0:T(8,128)} %get-tuple-element.20), custom_call_target="InvertDiagBlocksLowerTriangular" | custom-call | tf_op jit(solution)/shard_map/jit(_solve_triangular)/triangular_solve | solution.py:26
  435.4 2.7 fusion.4
  438.1 0.8 copy.22
  439.0 163.1 %all-reduce.3.cloned.1.call-done = f32[256,512]{1,0:T(8,128)} async-done(((f32[256,512]{1,0:T(8,128)}), f32[256,512]{1,0:T(8,128)}) %all-reduce.3.cloned.1.call-update) | async-done | bytes 524304 | tf_op jit(solution)/shard_map/psum | solution.py:54
  602.1 4.4 convolution_subtract_fusion
  606.5 0.8 copy.71
  (117 shorter events, 26.5 us)
Async XLA Ops:
  7.2 47.8 %all-gather.2.cloned.1.call-start = ((), (), s32[]{:S(2)}) async-start(), calls=%async_computation | async-start | bytes 1114112 | tf_op jit(solution)/shard_map/all_gather | solution.py:47
  7.9 594.2 %all-reduce.3.cloned.1.call-start = ((), (), s32[]{:S(2)}) async-start(), calls=%async_computation.1 | async-start | bytes 1048576 | tf_op jit(solution)/shard_map/psum | solution.py:54
  57.5 60.4 %copy-start = (f32[1024,256]{0,1:T(8,128)S(1)}, f32[1024,256]{0,1:T(8,128)}, u32[]{:S(2)}) copy-start(f32[1024,256]{0,1:T(8,128)} %all-gather.2.cloned.1.call-done) | copy-start | bytes 3145732
  158.1 12.8 %collective-permute-start = (f32[256,256]{1,0:T(8,128)S(1)}, f32[256,256]{1,0:T(8,128)S(1)}, u32[]{:S(2)}, u32[]{:S(2)}) collective-permute-start(f32[256,256]{1,0:T(8,128)S(1)} %fusion.24), channel_id=1, source_target_pairs={{16,0},{32,16},{48,32},{64,48},{80,64},{96,80},{112,96},{128,112},... | collective-permute-start | bytes 786440 | tf_op jit(solution)/shard_map/ppermute | solution.py:12
  208.1 14.4 %collective-permute-start.1 = (f32[256,256]{0,1:T(8,128)S(1)}, f32[256,256]{0,1:T(8,128)S(1)}, u32[]{:S(2)}, u32[]{:S(2)}) collective-permute-start(f32[256,256]{0,1:T(8,128)S(1)} %fusion.36), channel_id=1, source_target_pairs={{32,0},{48,16},{64,32},{80,48},{96,64},{112,80},{128,96},{144,112}... | collective-permute-start | bytes 786440 | tf_op jit(solution)/shard_map/ppermute | solution.py:12
  259.6 14.9 %collective-permute-start.2 = (f32[256,256]{0,1:T(8,128)S(1)}, f32[256,256]{0,1:T(8,128)S(1)}, u32[]{:S(2)}, u32[]{:S(2)}) collective-permute-start(f32[256,256]{0,1:T(8,128)S(1)} %fusion.33), channel_id=1, source_target_pairs={{64,0},{80,16},{96,32},{112,48},{128,64},{144,80},{160,96},{176,11... | collective-permute-start | bytes 786440 | tf_op jit(solution)/shard_map/ppermute | solution.py:12
  311.6 10.2 %collective-permute-start.3 = (f32[256,256]{0,1:T(8,128)S(1)}, f32[256,256]{0,1:T(8,128)S(1)}, u32[]{:S(2)}, u32[]{:S(2)}) collective-permute-start(f32[256,256]{0,1:T(8,128)S(1)} %fusion.30), channel_id=1, source_target_pairs={{128,0},{144,16},{160,32},{176,48},{192,64},{208,80},{224,96},{240... | collective-permute-start | bytes 786440 | tf_op jit(solution)/shard_map/ppermute | solution.py:12
  358.8 10.0 %collective-permute-start.4 = (f32[256,256]{0,1:T(8,128)S(1)}, f32[256,256]{0,1:T(8,128)S(1)}, u32[]{:S(2)}, u32[]{:S(2)}) collective-permute-start(f32[256,256]{0,1:T(8,128)S(1)} %fusion.27), channel_id=1, source_target_pairs={{256,0},{272,16},{288,32},{304,48},{320,64},{336,80},{352,96},{368... | collective-permute-start | bytes 786440 | tf_op jit(solution)/shard_map/ppermute | solution.py:12
  412.8 22.5 %copy-start.1 = (f32[1024,512]{1,0:T(8,128)S(1)}, f32[1024,512]{1,0:T(8,128)}, u32[]{:S(2)}) copy-start(f32[1024,512]{1,0:T(8,128)} %param.6) | copy-start | bytes 6291460
  434.1 1.2 copy-start.2
  435.4 2.8 copy-start.4
  602.1 4.4 copy-start.3
Sparse Core Ops, SparseCore 0:
  10.1 44.8 all-gather.1
  438.2 163.8 all-reduce.2
where the time goes:
time: 625 us; the launch traced here: 615 us
  other arithmetic  283 us (45%)
  waiting for transfers between devices  247 us (40%)
  between operations  24.3 us (4%)
  starting transfers between devices  24 us (4%)
  matrix products  22.8 us (4%)
  local copies, waits for them, and re-layouts  12.8 us (2%)
    another operation x35, other arithmetic, stacked_factor(): return jnp.linalg.cholesky(joined_gram).T  173 us
    psum x1, waiting for transfers between devices, shards(): coupling = lax.psum(inner_gram(q_local, trailing), 'row')  163 us
    another operation x13, other arithmetic, factor_pass(): chol_lower = jnp.linalg.cholesky(gram_mat)  68.8 us
    all_gather x1, waiting for transfers between devices, shards(): full_panel = lax.all_gather(panel_block, 'col', axis=1, tiled=True)  47 us
    another operation x5, other arithmetic, solve_lower(): return jax.scipy.linalg.solve_triangular(lower_mat, matrix.T, lower=True).T  41.4 us
    ppermute x5, waiting for transfers between devices, passed_along(): return lax.ppermute(block, axis, route)  36.1 us
    ppermute x5, starting transfers between devices, passed_along(): return lax.ppermute(block, axis, route)  24 us
  transfers between devices with their start and end apart: 7, of which 7 were waited for; matrix products, arithmetic and copies ran while one was open for 1% of the time, Pallas kernels for 0%

commit v1 on v0

v1 whole, which is shorter than its diff:
```python
import functools

import jax
import jax.numpy as jnp
from jax import lax
from jax.experimental import pallas as pl
from jax.experimental.pallas import tpu as pltpu
from jax.sharding import PartitionSpec as P

HIGHEST = lax.Precision.HIGHEST
MESH = pl.DeviceIdType.MESH
F32 = jnp.float32
B = 256
NB = 32
GRID_X = {32: 4, 4: 2}


def dot(left, right, left_dim, right_dim):
    return lax.dot_general(
        left, right, (((left_dim,), (right_dim,)), ((), ())), precision=HIGHEST, preferred_element_type=F32
    )


def eliminate_panel(tiles, rows):
    sublane = lax.broadcasted_iota(jnp.int32, (8, 128), 0)
    count = rows // 8
    column = {}
    for c in range(rows):
        for t in range(c // 8, count):
            column[c, t] = jnp.broadcast_to(tiles[t][0][:, c : c + 1], (8, 128))

    def spread(tile, s):
        return jnp.broadcast_to(tile[s : s + 1, :], (8, 128))

    pivots = [jnp.ones((8, 128), F32) for _ in range(count)]
    pivot = spread(column[0, 0], 0)
    for j in range(rows):
        tj, sj = divmod(j, 8)
        inverse = 1.0 / pivot
        pivots[tj] = jnp.where(sublane == sj, pivot, pivots[tj])
        along = {c: spread(column[j, c // 8], c % 8) for c in range(j + 1, rows)}
        if j + 1 < rows:
            tn, sn = divmod(j + 1, 8)
            pivot = spread(column[j + 1, tn], sn) - (along[j + 1] * along[j + 1]) * inverse
        for t in range(tj, count):
            factor = column[j, t] * inverse
            if t == tj:
                factor = jnp.where(sublane > sj, factor, 0.0)
            for c in range(j + 1, min(rows, 8 * t + 8)):
                column[c, t] = column[c, t] - factor * along[c]
            for w in range(len(tiles[t])):
                row = spread(tiles[tj][w], sj) if t > tj or sj < 7 else None
                if row is not None:
                    tiles[t][w] = tiles[t][w] - factor * row
    scales = []
    for value in pivots:
        scale = lax.rsqrt(value)
        scales.append(scale * (1.5 - 0.5 * value * scale * scale))
    return jnp.concatenate(
        [jnp.concatenate([piece * scale for piece in line], axis=1) for line, scale in zip(tiles, scales)], axis=0
    )


def kernel(
    nx, ny, nz,
    panel_ref, trailing_hbm,
    r_ref, coupling_ref, updated_hbm,
    pt, trail, gpart, grecv, gx, gall, schur, factors, wpart, wxrecv, wquarter, wyrecv, wall,
    local_sem, z_send, z_recv, p_send, p_recv, gy_send, gy_recv, gx_send, gx_recv, ga_send, ga_recv, gp_send, gp_recv,
    wx_send, wx_recv, wy_send, wy_recv, wa_send, wa_recv, wb_send, wb_recv,
):
    row, col = lax.axis_index("row"), lax.axis_index("col")
    x, y = row // ny, lax.rem(row, ny)
    z, core = col // 2, lax.rem(col, 2)
    half_z = nz // 2
    unit, rows = pt.shape[1], pt.shape[2]

    def at_x(d):
        return (lax.rem(x + d, nx) * ny + y, col)

    def at_y(d):
        return (x * ny + lax.rem(y + d, ny), col)

    def at_z(d):
        return (row, lax.rem(z + d + nz, nz) * 2 + core)

    partner = (row, z * 2 + 1 - core)

    load = pltpu.make_async_copy(trailing_hbm, trail, local_sem.at[0])
    load.start()

    barrier = pltpu.get_barrier_semaphore()
    peers = [partner, at_z(1), at_z(-1)] + [at_x(d) for d in range(1, nx)] + [at_y(d) for d in range(1, ny)]
    for peer in peers:
        pl.semaphore_signal(barrier, inc=1, device_id=peer, device_id_type=MESH)
    flipped = panel_ref[...].T
    for h in range(2):
        pt[col * 2 + h] = flipped[h * unit : (h + 1) * unit, :]
    pl.semaphore_wait(barrier, len(peers))

    sent = []

    def send(src, dst, send_sem, recv_sem, device):
        copy = pltpu.make_async_remote_copy(
            src_ref=src, dst_ref=dst, send_sem=send_sem, recv_sem=recv_sem, device_id=device, device_id_type=MESH
        )
        return copy

    def launch(copy):
        copy.start()
        sent.append(copy)
        return copy

    def z_copy(direction, s, h):
        source = lax.rem(z - direction * (s - 1) + nz, nz) * 2 + core
        way = 0 if direction == 1 else 1
        slot = pt.at[source * 2 + h]
        index = ((s - 1) * 2 + h) * 2 + way
        return send(slot, slot, z_send.at[index], z_recv.at[index], at_z(direction))

    def p_copy(offset, h):
        source = lax.rem(z - offset + nz, nz) * 2 + core
        slot = pt.at[source * 2 + h]
        index = (offset % nz) * 2 + h
        return send(slot, slot, p_send.at[index], p_recv.at[index], partner)

    def parts(direction, s):
        if s < half_z:
            return (0, 1)
        return (0,) if direction == 1 else (1,)

    for h in range(2):
        for direction in (1, -1):
            if h in parts(direction, 1):
                launch(z_copy(direction, 1, h))
    for h in range(2):
        launch(p_copy(0, h))
    for s in range(1, half_z + 1):
        for h in range(2):
            for direction in (1, -1):
                if h in parts(direction, s):
                    z_copy(direction, s, h).wait_recv()
                    if s < half_z and h in parts(direction, s + 1):
                        launch(z_copy(direction, s + 1, h))
                    launch(p_copy(direction * s, h))
    for offset in range(nz):
        for h in range(2):
            p_copy(offset, h).wait_recv()

    units = B // unit
    mine = pt[pl.ds(core * (units // 2), units // 2)].reshape(B // 2, rows)
    strip = pt[pl.ds(core * (units // 4), units // 4)].reshape(B // 4, rows)
    right = pt[units // 2 :].reshape(B // 2, rows)
    depth = gpart.shape[1]
    gram = jnp.concatenate([dot(mine, mine, 1, 1), dot(strip, right, 1, 1)], axis=0)
    gpart[...] = gram.reshape(gpart.shape)

    y_order = sorted(range(1, ny), key=lambda d: -min(d, ny - d))

    def gy_copy(d):
        return send(
            gpart.at[lax.rem(y + d, ny)], grecv.at[d - 1], gy_send.at[d - 1], gy_recv.at[d - 1], at_y(d)
        )

    for d in y_order:
        launch(gy_copy(d))

    load.wait()
    quarter = B // nx
    whole = pt[...].reshape(B, rows)
    wpart[...] = dot(whole, trail[...], 1, 0).reshape(wpart.shape)

    def wx_copy(d):
        return send(
            wpart.at[lax.rem(x + d, nx)], wxrecv.at[d - 1], wx_send.at[d - 1], wx_recv.at[d - 1], at_x(d)
        )

    x_order = sorted(range(1, nx), key=lambda d: -min(d, nx - d))

    for d in range(1, ny):
        gy_copy(d).wait_recv()
    total = gpart[y]
    for d in range(1, ny):
        total = total + grecv[d - 1]
    gx[x] = total

    def gx_copy(d):
        return send(gx.at[x], gx.at[x], gx_send.at[d - 1], gx_recv.at[d - 1], at_x(d))

    for d in x_order:
        launch(gx_copy(d))
    for d in x_order:
        launch(wx_copy(d))
    for d in range(1, nx):
        gx_copy(d).wait_recv()
    total = gx[0]
    for i in range(1, nx):
        total = total + gx[i]
    gall[core, y] = total

    def ga_copy(d):
        return send(gall.at[core, y], gall.at[core, y], ga_send.at[d - 1], ga_recv.at[d - 1], at_y(d))

    def gp_copy(d):
        slot = gall.at[core, lax.rem(y - d + ny, ny)]
        return send(slot, slot, gp_send.at[d], gp_recv.at[d], partner)

    for d in y_order:
        launch(ga_copy(d))
    launch(gp_copy(0))
    for d in reversed(y_order):
        ga_copy(d).wait_recv()
        launch(gp_copy(d))
    for d in range(ny):
        gp_copy(d).wait_recv()

    half = B // 2
    first = gall[0].reshape(ny * depth, half)
    second = gall[1].reshape(ny * depth, half)
    schur[0:half, 0:half] = first[0:half]
    schur[0 : half // 2, half:B] = first[half:]
    schur[half // 2 : half, half:B] = second[half:]
    schur[half:B, half:B] = second[0:half]
    schur[half:B, 0:half] = jnp.zeros((half, half), F32)
    steps = B // NB

    def wy_copy(d):
        return send(
            wquarter.at[lax.rem(y + d, ny)], wyrecv.at[d - 1], wy_send.at[d - 1], wy_recv.at[d - 1], at_y(d)
        )

    def wa_copy(d):
        return send(wall.at[x, y], wall.at[x, y], wa_send.at[d - 1], wa_recv.at[d - 1], at_y(d))

    def wb_copy(d):
        return send(wall.at[x], wall.at[x], wb_send.at[d - 1], wb_recv.at[d - 1], at_x(d))

    def sum_x():
        for d in range(1, nx):
            wx_copy(d).wait_recv()
        value = wpart[x]
        for d in range(1, nx):
            value = value + wxrecv[d - 1]
        wquarter[...] = value
        for d in y_order:
            wy_copy(d).start()

    def sum_y():
        for d in range(1, ny):
            wy_copy(d).wait_recv()
        value = wquarter[y]
        for d in range(1, ny):
            value = value + wyrecv[d - 1]
        wall[x, y] = value
        for d in y_order:
            wa_copy(d).start()

    def spread_x():
        for d in range(1, ny):
            wa_copy(d).wait_recv()
        for d in x_order:
            wb_copy(d).start()

    identity = (
        lax.broadcasted_iota(jnp.int32, (NB, half), 0) == lax.broadcasted_iota(jnp.int32, (NB, half), 1)
    ).astype(F32)

    def step(k, carry):
        top = jnp.concatenate([schur[0:NB, :], identity], axis=1)
        tiles = [[top[8 * t : 8 * t + 8, 128 * w : 128 * w + 128] for w in range(3)] for t in range(NB // 8)]
        lines = eliminate_panel(tiles, NB)
        wide = jnp.concatenate([lines, jnp.zeros((NB, half), F32)], axis=1)
        factors[pl.ds(pl.multiple_of(k * NB, NB), NB), :] = pltpu.roll(wide, k * NB, 1)
        change = dot(lines[:, 0:B], lines, 0, 0)
        rest = jnp.concatenate([schur[NB:B, :], jnp.zeros((B - NB, half), F32)], axis=1) - change[NB:B, :]
        schur[0 : B - NB, :] = pltpu.roll(rest, 3 * half - NB, 1)[:, 0:B]
        for at, stage in ((0, sum_x), (2, sum_y), (4, spread_x)):
            pl.when(k == at)(stage)
        return carry

    lax.fori_loop(0, steps, step, 0)

    upper = lax.broadcasted_iota(jnp.int32, (B, B), 0) <= lax.broadcasted_iota(jnp.int32, (B, B), 1)
    r_ref[...] = jnp.where(upper, factors[:, 0:B], 0.0)
    inverse = factors[:, B : 2 * B]
    for d in range(1, nx):
        wb_copy(d).wait_recv()
    columns = wall.shape[-1]
    coupling = dot(inverse, wall[...].reshape(B, columns), 1, 0)
    coupling_ref[...] = coupling
    weights = dot(inverse, coupling, 0, 0)
    block = 128
    stores = []
    for i in range(rows // block):
        part = pt[:, :, i * block : (i + 1) * block].reshape(B, block)
        trail[i * block : (i + 1) * block, :] = trail[i * block : (i + 1) * block, :] - dot(part, weights, 0, 0)
        store = pltpu.make_async_copy(
            trail.at[pl.ds(i * block, block)], updated_hbm.at[pl.ds(i * block, block)], local_sem.at[1 + i]
        )
        store.start()
        stores.append(store)
    for copy in sent:
        copy.wait_send()
    for d in range(1, ny):
        wy_copy(d).wait_send()
        wa_copy(d).wait_send()
    for d in range(1, nx):
        wb_copy(d).wait_send()
    for store in stores:
        store.wait()


def solution(mesh):
    nrow, ncol = mesh.shape["row"], mesh.shape["col"]
    nx = GRID_X[nrow]
    ny, nz = nrow // nx, ncol // 2

    def shard(panel, trailing):
        rows, width = panel.shape
        columns = trailing.shape[1]
        unit = width // 2
        depth = 3 * B // 4 // ny
        deep = B // nx // ny
        dma = pltpu.SemaphoreType.DMA
        return pl.pallas_call(
            functools.partial(kernel, nx, ny, nz),
            out_shape=(
                jax.ShapeDtypeStruct((B, B), F32),
                jax.ShapeDtypeStruct((B, columns), F32),
                jax.ShapeDtypeStruct((rows, columns), F32),
            ),
            in_specs=[pl.BlockSpec(memory_space=pltpu.VMEM), pl.BlockSpec(memory_space=pl.ANY)],
            out_specs=(
                pl.BlockSpec(memory_space=pltpu.VMEM),
                pl.BlockSpec(memory_space=pltpu.VMEM),
                pl.BlockSpec(memory_space=pl.ANY),
            ),
            scratch_shapes=[
                pltpu.VMEM((B // unit, unit, rows), F32),
                pltpu.VMEM((rows, columns), F32),
                pltpu.VMEM((ny, depth, B // 2), F32),
                pltpu.VMEM((ny - 1, depth, B // 2), F32),
                pltpu.VMEM((nx, depth, B // 2), F32),
                pltpu.VMEM((2, ny, depth, B // 2), F32),
                pltpu.VMEM((B, B), F32),
                pltpu.VMEM((B, 2 * B), F32),
                pltpu.VMEM((nx, ny, deep, columns), F32),
                pltpu.VMEM((nx - 1, ny, deep, columns), F32),
                pltpu.VMEM((ny, deep, columns), F32),
                pltpu.VMEM((ny - 1, deep, columns), F32),
                pltpu.VMEM((nx, ny, deep, columns), F32),
                dma((1 + rows // 128,)),
                dma((2 * nz,)), dma((2 * nz,)),
                dma((2 * nz,)), dma((2 * nz,)),
                dma((ny - 1,)), dma((ny - 1,)),
                dma((nx - 1,)), dma((nx - 1,)),
                dma((ny - 1,)), dma((ny - 1,)),
                dma((ny,)), dma((ny,)),
                dma((nx - 1,)), dma((nx - 1,)),
                dma((ny - 1,)), dma((ny - 1,)),
                dma((ny - 1,)), dma((ny - 1,)),
                dma((nx - 1,)), dma((nx - 1,)),
            ],
            compiler_params=pltpu.CompilerParams(
                collective_id=0, has_side_effects=True, vmem_limit_bytes=48 * 1024 * 1024
            ),
        )(panel, trailing)

    return jax.shard_map(
        shard,
        mesh=mesh,
        in_specs=(P("row", "col"), P("row", "col")),
        out_specs=(P(), P(None, "col"), P("row", "col")),
        check_vma=False,
    )
```

time: 625 us -> 76.5 us (0.12)
  the two profiles are of different devices: /device:TPU:64 before, /device:TPU:1 now
where the time goes in v1:
time: 76.5 us; the launch traced here: 76.3 us
  Pallas kernels  70.2 us (92%)
  local copies, waits for them, and re-layouts  5.44 us (7%)
    pallas_call x1, Pallas kernels, shard(): pl.pallas_call(functools.partial(kernel, nx, ny, nz), out_shape=(jax.Shap...  70.2 us
    unnamed x6, local copies, waits for them, and re-layouts  5.44 us

profile of v1, /device:TPU:1, one launch (start us, length us, event | category | flops | bytes accessed | tf_op | source)
XLA Modules:
  0.0 76.3 jit_solution(1422752262273437980)
XLA Ops:
  0.6 1.0 %copy.5.panel_ref = f32[1024,16]{1,0:T(8,128)S(1)} copy(f32[1024,16]{0,1:T(8,128)} %param.2) | data formatting | bytes 131072 | tf_op args[0]
  1.7 0.0 copy-start
  1.7 1.6 %copy-done = f32[1024,512]{1,0:T(8,128)S(1)} copy-done((f32[1024,512]{1,0:T(8,128)S(1)}, f32[1024,512]{1,0:T(8,128)}, u32[]{:S(2)}) %copy-start) | copy-done | bytes 2097176
  3.3 70.2 %shard_map.49 = (f32[256,256]{1,0:T(8,128)S(1)}, f32[256,512]{1,0:T(8,128)S(1)}, f32[1024,512]{1,0:T(8,128)S(1)}) custom-call(f32[1024,16]{1,0:T(8,128)S(1)} %copy.5.panel_ref, f32[1024,512]{1,0:T(8,128)S(1)} %copy-done), custom_call_target="tpu_custom_call" | custom-call | tf_op jit(solution)/shard_map/pallas_call | solution.py:325
  73.5 0.7 copy.9
  74.2 0.8 %copy.10 = f32[256,512]{1,0:T(8,128)} copy(f32[256,512]{1,0:T(8,128)S(1)} %get-tuple-element.7) | data formatting | bytes 1048576
  75.0 1.3 %copy.11 = f32[1024,512]{1,0:T(8,128)} copy(f32[1024,512]{1,0:T(8,128)S(1)} %get-tuple-element.8) | data formatting | bytes 4194304
Async XLA Ops:
  1.7 1.6 %copy-start = (f32[1024,512]{1,0:T(8,128)S(1)}, f32[1024,512]{1,0:T(8,128)}, u32[]{:S(2)}) copy-start(f32[1024,512]{1,0:T(8,128)} %trailing_hbm.1) | copy-start | bytes 6291460

commit v2 on v1

v2 whole, which is shorter than its diff:
```python
import functools

import jax
import jax.numpy as jnp
from jax import lax
from jax.experimental import pallas as pl
from jax.experimental.pallas import tpu as pltpu
from jax.sharding import PartitionSpec as P

HIGHEST = lax.Precision.HIGHEST
MESH = pl.DeviceIdType.MESH
F32 = jnp.float32
B = 256
NB = 32
GRID_X = {32: 4, 4: 2}


def dot(left, right, left_dim, right_dim):
    return lax.dot_general(
        left, right, (((left_dim,), (right_dim,)), ((), ())), precision=HIGHEST, preferred_element_type=F32
    )


def eliminate_panel(tiles, rows):
    sublane = lax.broadcasted_iota(jnp.int32, (8, 128), 0)
    count = rows // 8
    column = {}
    for c in range(rows):
        for t in range(c // 8, count):
            column[c, t] = jnp.broadcast_to(tiles[t][0][:, c : c + 1], (8, 128))

    def spread(tile, s):
        return jnp.broadcast_to(tile[s : s + 1, :], (8, 128))

    pivots = [jnp.ones((8, 128), F32) for _ in range(count)]
    pivot = spread(column[0, 0], 0)
    for j in range(rows):
        tj, sj = divmod(j, 8)
        inverse = 1.0 / pivot
        pivots[tj] = jnp.where(sublane == sj, pivot, pivots[tj])
        along = {c: spread(column[j, c // 8], c % 8) for c in range(j + 1, rows)}
        if j + 1 < rows:
            tn, sn = divmod(j + 1, 8)
            pivot = spread(column[j + 1, tn], sn) - (along[j + 1] * along[j + 1]) * inverse
        for t in range(tj, count):
            factor = column[j, t] * inverse
            if t == tj:
                factor = jnp.where(sublane > sj, factor, 0.0)
            for c in range(j + 1, min(rows, 8 * t + 8)):
                column[c, t] = column[c, t] - factor * along[c]
            for w in range(len(tiles[t])):
                row = spread(tiles[tj][w], sj) if t > tj or sj < 7 else None
                if row is not None:
                    tiles[t][w] = tiles[t][w] - factor * row
    scales = []
    for value in pivots:
        scale = lax.rsqrt(value)
        scales.append(scale * (1.5 - 0.5 * value * scale * scale))
    return jnp.concatenate(
        [jnp.concatenate([piece * scale for piece in line], axis=1) for line, scale in zip(tiles, scales)], axis=0
    )


def kernel(
    nx, ny, nz,
    panel_hbm, trailing_hbm,
    r_ref, coupling_ref, updated_hbm,
    pt, trail, gx, gy, gz, schur, factors, wpart, wxrecv, wquarter, wyrecv, wall,
    local_sem, z_send, z_recv, p_send, p_recv, send_sem, recv_sem,
):
    row, col = lax.axis_index("row"), lax.axis_index("col")
    x, y = row // ny, lax.rem(row, ny)
    z, core = col // 2, lax.rem(col, 2)
    ncol = 2 * nz
    width, rows = pt.shape[1], pt.shape[2]

    def at_x(d):
        return (lax.rem(x + d, nx) * ny + y, col)

    def at_y(d):
        return (x * ny + lax.rem(y + d, ny), col)

    def at_z(d, flip=False):
        return (row, lax.rem(z + d + nz, nz) * 2 + (1 - core if flip else core))

    partner = at_z(0, True)
    x_order = sorted(range(1, nx), key=lambda d: -min(d, nx - d))
    y_order = sorted(range(1, ny), key=lambda d: -min(d, ny - d))
    z_order = sorted(range(1, nz), key=lambda d: -min(d, nz - d))

    fetch = pltpu.make_async_copy(panel_hbm, pt.at[col], local_sem.at[1])
    fetch.start()
    load = pltpu.make_async_copy(trailing_hbm, trail, local_sem.at[0])
    load.start()

    barrier = pltpu.get_barrier_semaphore()
    peers = [partner] + [at_z(d, flip) for d in z_order for flip in (False, True)]
    peers += [at_x(d) for d in x_order] + [at_y(d) for d in y_order]
    for peer in peers:
        pl.semaphore_signal(barrier, inc=1, device_id=peer, device_id_type=MESH)
    fetch.wait()
    pl.semaphore_wait(barrier, len(peers))

    def remote(src, dst, send, recv, device):
        return pltpu.make_async_remote_copy(
            src_ref=src, dst_ref=dst, send_sem=send, recv_sem=recv, device_id=device, device_id_type=MESH
        )

    def await_bytes(ref, sem):
        pltpu.make_async_copy(ref, ref, sem).wait()

    def block(offset):
        return pt.at[lax.rem(z - offset + nz, nz) * 2 + core]

    def half_block(offset, h):
        return pt.at[lax.rem(z - offset + nz, nz) * 2 + core, pl.ds(h * (width // 2), width // 2)]

    gathered = []

    def launch(copy):
        copy.start()
        gathered.append(copy)

    def own_copy(d, i):
        return remote(block(0), block(0), z_send.at[i], z_recv.at[i], at_z(d))

    def pass_copy(d, i):
        return remote(block(2 * d), block(2 * d), z_send.at[i], z_recv.at[i], at_z(d))

    def half_copy(d, i):
        part = half_block(2 * d, 0 if d == 1 else 1)
        return remote(part, part, z_send.at[i], z_recv.at[i], at_z(2 * d))

    def partner_copy(offset, i):
        return remote(block(offset), block(offset), p_send.at[i], p_recv.at[i], partner)

    handed = [0]
    if nz == 8:
        for i, d in enumerate((2, -2, 1, -1)):
            launch(own_copy(d, i))
        launch(partner_copy(0, 0))
        for i, d in enumerate((2, -2)):
            own_copy(d, i).wait_recv()
            launch(half_copy(d // 2, 4 + i))
            launch(pass_copy(d // 2, 6 + i))
            launch(partner_copy(d, 1 + i))
            handed.append(d)
        for i, d in enumerate((1, -1)):
            own_copy(d, 2 + i).wait_recv()
            launch(partner_copy(d, 3 + i))
            handed.append(d)
        for i, d in enumerate((1, -1)):
            pass_copy(d, 6 + i).wait_recv()
            launch(partner_copy(3 * d, 5 + i))
            handed.append(3 * d)
        for i, d in enumerate((1, -1)):
            half_copy(d, 4 + i).wait_recv()
        launch(partner_copy(4, 7))
        handed.append(4)
    else:
        for i, d in enumerate(z_order):
            launch(own_copy(d, i))
        launch(partner_copy(0, 0))
        for i, d in enumerate(z_order):
            own_copy(d, i).wait_recv()
            launch(partner_copy(d, 1 + i))
            handed.append(d)
    for i, offset in enumerate(handed):
        partner_copy(offset, i).wait_recv()

    tiles = 48 // ncol
    per_block = width // 8
    pieces, lefts = [], []
    for i in range(tiles):
        t = col * tiles + i
        unit = jnp.where(t < 16, t, t - 16)
        lefts.append(t < 16)
        pieces.append(pt[unit // per_block, pl.ds(pl.multiple_of(lax.rem(unit, per_block) * 8, 8), 8), :])
    whole = pt[...].reshape(B, rows)
    gram = dot(jnp.concatenate(pieces, axis=0), whole, 1, 1)
    for i in range(tiles):
        line = gram[8 * i : 8 * i + 8, :]
        gx[x, i] = jnp.where(lefts[i], line[:, 0 : B // 2], line[:, B // 2 : B])

    def gx_copy(d):
        return remote(gx.at[x], gx.at[x], send_sem.at[0], recv_sem.at[0], at_x(d))

    def gy_copy(d):
        return remote(gy.at[y], gy.at[y], send_sem.at[1], recv_sem.at[1], at_y(d))

    def gz_copy(device):
        return remote(gz.at[col], gz.at[col], send_sem.at[2], recv_sem.at[2], device)

    def wx_copy(d):
        return remote(wpart.at[lax.rem(x + d, nx)], wxrecv.at[d - 1], send_sem.at[3], recv_sem.at[3], at_x(d))

    def wy_copy(d):
        return remote(wquarter.at[lax.rem(y + d, ny)], wyrecv.at[d - 1], send_sem.at[4], recv_sem.at[4], at_y(d))

    def wa_copy(h, d):
        return remote(wall.at[h, x, y], wall.at[h, x, y], send_sem.at[5 + h], recv_sem.at[5 + h], at_y(d))

    def wb_copy(h, d):
        return remote(wall.at[h, x], wall.at[h, x], send_sem.at[7 + h], recv_sem.at[7 + h], at_x(d))

    def sum_x():
        await_bytes(wxrecv, recv_sem.at[3])
        value = wpart[x]
        for d in range(1, nx):
            value = value + wxrecv[d - 1]
        wquarter[...] = value
        for d in y_order:
            wy_copy(d).start()

    columns = wpart.shape[-1]

    def sum_y():
        await_bytes(wyrecv, recv_sem.at[4])
        value = wquarter[y]
        for d in range(1, ny):
            value = value + wyrecv[d - 1]
        for h in range(2):
            wall[h, x, y] = value[:, h * (columns // 2) : (h + 1) * (columns // 2)]
        for h in range(2):
            for d in y_order:
                wa_copy(h, d).start()

    def spread_x(h):
        await_bytes(wall.at[h, 0, pl.ds(0, ny - 1)], recv_sem.at[5 + h])
        for d in x_order:
            wb_copy(h, d).start()

    for d in x_order:
        gx_copy(d).start()
    load.wait()
    wpart[...] = dot(whole, trail[...], 1, 0).reshape(wpart.shape)
    await_bytes(gx.at[pl.ds(0, nx - 1)], recv_sem.at[0])
    total = gx[0]
    for i in range(1, nx):
        total = total + gx[i]
    gy[y] = total
    for d in y_order:
        gy_copy(d).start()
    for d in x_order:
        wx_copy(d).start()
    await_bytes(gy.at[pl.ds(0, ny - 1)], recv_sem.at[1])
    total = gy[0]
    for i in range(1, ny):
        total = total + gy[i]
    gz[col] = total
    for d in z_order:
        gz_copy(at_z(d)).start()
        gz_copy(at_z(d, True)).start()
    gz_copy(partner).start()
    sum_x()
    await_bytes(gz.at[pl.ds(0, ncol - 1)], recv_sem.at[2])

    half = B // 2
    packed = gz[...].reshape(3 * half, half)
    schur[0:half, 0:half] = packed[0:half]
    schur[0:half, half:B] = packed[half:B]
    schur[half:B, half:B] = packed[B:]
    schur[half:B, 0:half] = jnp.zeros((half, half), F32)
    steps = B // NB

    identity = (
        lax.broadcasted_iota(jnp.int32, (NB, half), 0) == lax.broadcasted_iota(jnp.int32, (NB, half), 1)
    ).astype(F32)

    def step(k, carry):
        top = jnp.concatenate([schur[0:NB, :], identity], axis=1)
        tiles = [[top[8 * t : 8 * t + 8, 128 * w : 128 * w + 128] for w in range(3)] for t in range(NB // 8)]
        lines = eliminate_panel(tiles, NB)
        wide = jnp.concatenate([lines, jnp.zeros((NB, half), F32)], axis=1)
        factors[pl.ds(pl.multiple_of(k * NB, NB), NB), :] = pltpu.roll(wide, k * NB, 1)
        change = dot(lines[:, 0:B], lines, 0, 0)
        rest = jnp.concatenate([schur[NB:B, :], jnp.zeros((B - NB, half), F32)], axis=1) - change[NB:B, :]
        schur[0 : B - NB, :] = pltpu.roll(rest, 3 * half - NB, 1)[:, 0:B]
        for at, stage in ((0, sum_y), (3, lambda: spread_x(0)), (5, lambda: spread_x(1))):
            pl.when(k == at)(stage)
        return carry

    lax.fori_loop(0, steps, step, 0)

    upper = lax.broadcasted_iota(jnp.int32, (B, B), 0) <= lax.broadcasted_iota(jnp.int32, (B, B), 1)
    r_ref[...] = jnp.where(upper, factors[:, 0:B], 0.0)
    inverse = factors[:, B : 2 * B]
    for h in range(2):
        await_bytes(wall.at[h, pl.ds(0, nx - 1)], recv_sem.at[7 + h])
    summed = jnp.concatenate([wall[h].reshape(B, columns // 2) for h in range(2)], axis=1)
    coupling = dot(inverse, summed, 1, 0)
    coupling_ref[...] = coupling
    weights = dot(inverse, coupling, 0, 0)
    lines = 128
    stores = []
    for i in range(rows // lines):
        part = pt[:, :, i * lines : (i + 1) * lines].reshape(B, lines)
        trail[i * lines : (i + 1) * lines, :] = trail[i * lines : (i + 1) * lines, :] - dot(part, weights, 0, 0)
        store = pltpu.make_async_copy(
            trail.at[pl.ds(i * lines, lines)], updated_hbm.at[pl.ds(i * lines, lines)], local_sem.at[2 + i]
        )
        store.start()
        stores.append(store)
    for copy in gathered:
        copy.wait_send()
    await_bytes(gx.at[pl.ds(0, nx - 1)], send_sem.at[0])
    await_bytes(gy.at[pl.ds(0, ny - 1)], send_sem.at[1])
    await_bytes(gz.at[pl.ds(0, ncol - 1)], send_sem.at[2])
    await_bytes(wxrecv, send_sem.at[3])
    await_bytes(wyrecv, send_sem.at[4])
    for h in range(2):
        await_bytes(wall.at[h, 0, pl.ds(0, ny - 1)], send_sem.at[5 + h])
        await_bytes(wall.at[h, pl.ds(0, nx - 1)], send_sem.at[7 + h])
    for store in stores:
        store.wait()


def solution(mesh):
    nrow, ncol = mesh.shape["row"], mesh.shape["col"]
    nx = GRID_X[nrow]
    ny, nz = nrow // nx, ncol // 2

    def shard(panel, trailing):
        rows, width = panel.shape
        columns = trailing.shape[1]
        tiles = 48 // ncol
        deep = B // nx // ny
        dma = pltpu.SemaphoreType.DMA
        hops = max(nz, 8)
        return pl.pallas_call(
            functools.partial(kernel, nx, ny, nz),
            out_shape=(
                jax.ShapeDtypeStruct((B, B), F32),
                jax.ShapeDtypeStruct((B, columns), F32),
                jax.ShapeDtypeStruct((rows, columns), F32),
            ),
            in_specs=[pl.BlockSpec(memory_space=pltpu.HBM)] * 2,
            out_specs=(
                pl.BlockSpec(memory_space=pltpu.VMEM),
                pl.BlockSpec(memory_space=pltpu.VMEM),
                pl.BlockSpec(memory_space=pltpu.HBM),
            ),
            scratch_shapes=[
                pltpu.VMEM((ncol, width, rows), F32),
                pltpu.VMEM((rows, columns), F32),
                pltpu.VMEM((nx, tiles, 8, B // 2), F32),
                pltpu.VMEM((ny, tiles, 8, B // 2), F32),
                pltpu.VMEM((ncol, tiles, 8, B // 2), F32),
                pltpu.VMEM((B, B), F32),
                pltpu.VMEM((B, 2 * B), F32),
                pltpu.VMEM((nx, ny, deep, columns), F32),
                pltpu.VMEM((nx - 1, ny, deep, columns), F32),
                pltpu.VMEM((ny, deep, columns), F32),
                pltpu.VMEM((ny - 1, deep, columns), F32),
                pltpu.VMEM((2, nx, ny, deep, columns // 2), F32),
                dma((2 + rows // 128,)),
                dma((hops,)), dma((hops,)),
                dma((hops,)), dma((hops,)),
                dma((9,)), dma((9,)),
            ],
            compiler_params=pltpu.CompilerParams(
                collective_id=0, has_side_effects=True, vmem_limit_bytes=67_000_000
            ),
        )(panel.T, trailing)

    return jax.shard_map(
        shard,
        mesh=mesh,
        in_specs=(P("row", "col"), P("row", "col")),
        out_specs=(P(), P(None, "col"), P("row", "col")),
        check_vma=False,
    )
```

time: 76.5 us -> 67.2 us (0.88)
  Pallas kernels: 70.2 us -> 59.7 us
  local copies, waits for them, and re-layouts: 5.44 us -> 6.62 us
    pallas_call x1, Pallas kernels: 70.2 us -> 59.7 us  [shard(): pl.pallas_call(functools.partial(kernel, nx, ny, nz), out_shape=(jax.Shap...]
    unnamed x6 -> x3, local copies, waits for them, and re-layouts: 5.44 us -> 6.62 us
where the time goes in v2:
time: 67.2 us; the launch traced here: 67 us
  Pallas kernels  59.7 us (89%)
  local copies, waits for them, and re-layouts  6.62 us (10%)
    pallas_call x1, Pallas kernels, shard(): pl.pallas_call(functools.partial(kernel, nx, ny, nz), out_shape=(jax.Shap...  59.7 us
    unnamed x3, local copies, waits for them, and re-layouts  6.62 us

profile of v2, /device:TPU:1, one launch (start us, length us, event | category | flops | bytes accessed | tf_op | source)
XLA Modules:
  0.0 67.0 jit_solution(11504748523093720883)
XLA Ops:
  0.6 59.7 %shard_map.49 = (f32[256,256]{1,0:T(8,128)}, f32[256,512]{1,0:T(8,128)}, f32[1024,512]{1,0:T(8,128)}) custom-call(f32[16,1024]{1,0:T(8,128)} %bitcast.1, f32[1024,512]{1,0:T(8,128)} %trailing_hbm.1), custom_call_target="tpu_custom_call" | custom-call | tf_op jit(solution)/shard_map/pallas_call | solution.py:330
  60.3 1.7 %copy.8 = f32[256,256]{1,0:T(8,128)} copy(f32[256,256]{1,0:T(8,128)} %get-tuple-element.6) | data formatting | bytes 524288
  62.0 1.9 %copy.9 = f32[256,512]{1,0:T(8,128)} copy(f32[256,512]{1,0:T(8,128)} %get-tuple-element.7) | data formatting | bytes 1048576
  63.9 3.1 %copy.10 = f32[1024,512]{1,0:T(8,128)} copy(f32[1024,512]{1,0:T(8,128)} %get-tuple-element.8) | data formatting | bytes 4194304

commit v3 on v2

--- a/solution.py
+++ b/solution.py
@@ -64,8 +64,8 @@
 def kernel(
     nx, ny, nz,
     panel_hbm, trailing_hbm,
-    r_ref, coupling_ref, updated_hbm,
-    pt, trail, gx, gy, gz, schur, factors, wpart, wxrecv, wquarter, wyrecv, wall,
+    pt_ref, wall_ref, factors, trail,
+    pt, gx, gy, gz, schur, wpart, wxrecv, wquarter, wyrecv, wall,
     local_sem, z_send, z_recv, p_send, p_recv, send_sem, recv_sem,
 ):
     row, col = lax.axis_index("row"), lax.axis_index("col")
@@ -253,6 +253,7 @@
         gz_copy(at_z(d, True)).start()
     gz_copy(partner).start()
     sum_x()
+    pt_ref[...] = whole
     await_bytes(gz.at[pl.ds(0, ncol - 1)], recv_sem.at[2])
 
     half = B // 2
@@ -282,25 +283,9 @@
 
     lax.fori_loop(0, steps, step, 0)
 
-    upper = lax.broadcasted_iota(jnp.int32, (B, B), 0) <= lax.broadcasted_iota(jnp.int32, (B, B), 1)
-    r_ref[...] = jnp.where(upper, factors[:, 0:B], 0.0)
-    inverse = factors[:, B : 2 * B]
     for h in range(2):
         await_bytes(wall.at[h, pl.ds(0, nx - 1)], recv_sem.at[7 + h])
-    summed = jnp.concatenate([wall[h].reshape(B, columns // 2) for h in range(2)], axis=1)
-    coupling = dot(inverse, summed, 1, 0)
-    coupling_ref[...] = coupling
-    weights = dot(inverse, coupling, 0, 0)
-    lines = 128
-    stores = []
-    for i in range(rows // lines):
-        part = pt[:, :, i * lines : (i + 1) * lines].reshape(B, lines)
-        trail[i * lines : (i + 1) * lines, :] = trail[i * lines : (i + 1) * lines, :] - dot(part, weights, 0, 0)
-        store = pltpu.make_async_copy(
-            trail.at[pl.ds(i * lines, lines)], updated_hbm.at[pl.ds(i * lines, lines)], local_sem.at[2 + i]
-        )
-        store.start()
-        stores.append(store)
+        wall_ref[:, h * (columns // 2) : (h + 1) * (columns // 2)] = wall[h].reshape(B, columns // 2)
     for copy in gathered:
         copy.wait_send()
     await_bytes(gx.at[pl.ds(0, nx - 1)], send_sem.at[0])
@@ -311,6 +296,27 @@
     for h in range(2):
         await_bytes(wall.at[h, 0, pl.ds(0, ny - 1)], send_sem.at[5 + h])
         await_bytes(wall.at[h, pl.ds(0, nx - 1)], send_sem.at[7 + h])
+
+
+def update_kernel(pt, summed, factors, trail, r_hbm, coupling_hbm, updated_hbm, r_out, coupling_out, out, sems):
+    rows = trail.shape[0]
+    upper = lax.broadcasted_iota(jnp.int32, (B, B), 0) <= lax.broadcasted_iota(jnp.int32, (B, B), 1)
+    r_out[...] = jnp.where(upper, factors[:, 0:B], 0.0)
+    stores = [pltpu.make_async_copy(r_out, r_hbm, sems.at[0])]
+    stores[0].start()
+    inverse = factors[:, B : 2 * B]
+    coupling = dot(inverse, summed[...], 1, 0)
+    coupling_out[...] = coupling
+    stores.append(pltpu.make_async_copy(coupling_out, coupling_hbm, sems.at[1]))
+    stores[1].start()
+    weights = dot(inverse, coupling, 0, 0)
+    lines = 128
+    for i in range(rows // lines):
+        part = pt[:, i * lines : (i + 1) * lines]
+        span = pl.ds(i * lines, lines)
+        out[span, :] = trail[span, :] - dot(part, weights, 0, 0)
+        stores.append(pltpu.make_async_copy(out.at[span], updated_hbm.at[span], sems.at[2 + i]))
+        stores[-1].start()
     for store in stores:
         store.wait()
 
@@ -327,41 +333,55 @@
         deep = B // nx // ny
         dma = pltpu.SemaphoreType.DMA
         hops = max(nz, 8)
+        panel_t, summed, factors, trail = pl.pallas_call(
+            functools.partial(kernel, nx, ny, nz),
+            out_shape=(
+                jax.ShapeDtypeStruct((B, rows), F32),
+                jax.ShapeDtypeStruct((B, columns), F32),
+                jax.ShapeDtypeStruct((B, 2 * B), F32),
+                jax.ShapeDtypeStruct((rows, columns), F32),
+            ),
+            in_specs=[pl.BlockSpec(memory_space=pltpu.HBM)] * 2,
+            out_specs=(pl.BlockSpec(memory_space=pltpu.VMEM),) * 4,
+            scratch_shapes=[
+                pltpu.VMEM((ncol, width, rows), F32),
+                pltpu.VMEM((nx, tiles, 8, B // 2), F32),
+                pltpu.VMEM((ny, tiles, 8, B // 2), F32),
+                pltpu.VMEM((ncol, tiles, 8, B // 2), F32),
+                pltpu.VMEM((B, B), F32),
+                pltpu.VMEM((nx, ny, deep, columns), F32),
+                pltpu.VMEM((nx - 1, ny, deep, columns), F32),
+                pltpu.VMEM((ny, deep, columns), F32),
+                pltpu.VMEM((ny - 1, deep, columns), F32),
+                pltpu.VMEM((2, nx, ny, deep, columns // 2), F32),
+                dma((2,)),
+                dma((hops,)), dma((hops,)),
+                dma((hops,)), dma((hops,)),
+                dma((9,)), dma((9,)),
+            ],
+            compiler_params=pltpu.CompilerParams(
+                collective_id=0, has_side_effects=True, vmem_limit_bytes=48 * 1024 * 1024
+            ),
+        )(
+            pltpu.with_memory_space_constraint(panel.T, pltpu.HBM), pltpu.with_memory_space_constraint(trailing, pltpu.HBM)
+        )
         return pl.pallas_call(
-            functools.partial(kernel, nx, ny, nz),
+            update_kernel,
             out_shape=(
                 jax.ShapeDtypeStruct((B, B), F32),
                 jax.ShapeDtypeStruct((B, columns), F32),
                 jax.ShapeDtypeStruct((rows, columns), F32),
             ),
-            in_specs=[pl.BlockSpec(memory_space=pltpu.HBM)] * 2,
-            out_specs=(
-                pl.BlockSpec(memory_space=pltpu.VMEM),
-                pl.BlockSpec(memory_space=pltpu.VMEM),
-                pl.BlockSpec(memory_space=pltpu.HBM),
-            ),
+            in_specs=[pl.BlockSpec(memory_space=pltpu.VMEM)] * 4,
+            out_specs=(pl.BlockSpec(memory_space=pltpu.HBM),) * 3,
             scratch_shapes=[
-                pltpu.VMEM((ncol, width, rows), F32),
+                pltpu.VMEM((B, B), F32),
+                pltpu.VMEM((B, columns), F32),
                 pltpu.VMEM((rows, columns), F32),
-                pltpu.VMEM((nx, tiles, 8, B // 2), F32),
-                pltpu.VMEM((ny, tiles, 8, B // 2), F32),
-                pltpu.VMEM((ncol, tiles, 8, B // 2), F32),
-                pltpu.VMEM((B, B), F32),
-                pltpu.VMEM((B, 2 * B), F32),
-                pltpu.VMEM((nx, ny, deep, columns), F32),
-                pltpu.VMEM((nx - 1, ny, deep, columns), F32),
-                pltpu.VMEM((ny, deep, columns), F32),
-                pltpu.VMEM((ny - 1, deep, columns), F32),
-                pltpu.VMEM((2, nx, ny, deep, columns // 2), F32),
                 dma((2 + rows // 128,)),
-                dma((hops,)), dma((hops,)),
-                dma((hops,)), dma((hops,)),
-                dma((9,)), dma((9,)),
             ],
-            compiler_params=pltpu.CompilerParams(
-                collective_id=0, has_side_effects=True, vmem_limit_bytes=67_000_000
-            ),
-        )(panel.T, trailing)
+            compiler_params=pltpu.CompilerParams(vmem_limit_bytes=32 * 1024 * 1024),
+        )(panel_t, summed, factors, trail)
 
     return jax.shard_map(
         shard,

time: 67.2 us -> 59.7 us (0.89)
  local copies, waits for them, and re-layouts: 6.62 us -> 0 us
  Pallas kernels: 59.7 us -> 58.9 us
    unnamed x3 -> x0, local copies, waits for them, and re-layouts: 6.62 us -> none
    pallas_call x1, Pallas kernels: 59.7 us -> 55 us  [shard(): pl.pallas_call(functools.partial(kernel, nx, ny, nz), out_shape=(jax.Shap...]
    pallas_call x0 -> x1, Pallas kernels: none -> 3.88 us  [shard(): pl.pallas_call(update_kernel, out_shape=(jax.ShapeDtypeStruct((B, B), F32...]
where the time goes in v3:
time: 59.7 us; the launch traced here: 59.6 us
  Pallas kernels  58.9 us (99%)
  between operations  0.64 us (1%)
    pallas_call x1, Pallas kernels, shard(): pl.pallas_call(functools.partial(kernel, nx, ny, nz), out_shape=(jax.Shap...  55 us
    pallas_call x1, Pallas kernels, shard(): pl.pallas_call(update_kernel, out_shape=(jax.ShapeDtypeStruct((B, B), F32...  3.88 us

profile of v3, /device:TPU:1, one launch (start us, length us, event | category | flops | bytes accessed | tf_op | source)
XLA Modules:
  0.0 59.6 jit_solution(14005184653092654880)
XLA Ops:
  0.6 55.0 %shard_map.49 = (f32[256,1024]{1,0:T(8,128)S(1)}, f32[256,512]{1,0:T(8,128)S(1)}, f32[256,512]{1,0:T(8,128)S(1)}, f32[1024,512]{1,0:T(8,128)S(1)}) custom-call(f32[16,1024]{1,0:T(8,128)} %bitcast.1, f32[1024,512]{1,0:T(8,128)} %trailing_hbm.1), custom_call_target="tpu_custom_call" | custom-call | tf_op jit(solution)/shard_map/pallas_call | solution.py:336
  55.7 3.9 %shard_map.50 = (f32[256,256]{1,0:T(8,128)}, f32[256,512]{1,0:T(8,128)}, f32[1024,512]{1,0:T(8,128)}) custom-call(f32[256,1024]{1,0:T(8,128)S(1)} %get-tuple-element.7.pt, f32[256,512]{1,0:T(8,128)S(1)} %get-tuple-element.8.summed, f32[256,512]{1,0:T(8,128)S(1)} %get-tuple-element.9.factors, f32[1024,512]{1,0:T(8,128)S(1)} %get-tuple-element.10.trail), custom_call_target="tpu_custom_call" | custom-call | tf_op jit(solution)/shard_map/pallas_call | solution.py:368

commit v4 on v3

--- a/solution.py
+++ b/solution.py
@@ -10,6 +10,7 @@
 HIGHEST = lax.Precision.HIGHEST
 MESH = pl.DeviceIdType.MESH
 F32 = jnp.float32
+BF16 = jnp.bfloat16
 B = 256
 NB = 32
 GRID_X = {32: 4, 4: 2}
@@ -18,6 +19,30 @@
 def dot(left, right, left_dim, right_dim):
     return lax.dot_general(
         left, right, (((left_dim,), (right_dim,)), ((), ())), precision=HIGHEST, preferred_element_type=F32
+    )
+
+
+def mxu(left, right, left_dim, right_dim):
+    return lax.dot_general(left, right, (((left_dim,), (right_dim,)), ((), ())), preferred_element_type=F32)
+
+
+def split(value):
+    high = value.astype(BF16)
+    return high, (value - high.astype(F32)).astype(BF16)
+
+
+def split3(value):
+    high = value.astype(BF16)
+    rest = value - high.astype(F32)
+    middle = rest.astype(BF16)
+    return high, middle, (rest - middle.astype(F32)).astype(BF16)
+
+
+def dot3(left, right, left_dim, right_dim):
+    return (
+        mxu(left[0], right[1], left_dim, right_dim)
+        + mxu(left[1], right[0], left_dim, right_dim)
+        + mxu(left[0], right[0], left_dim, right_dim)
     )
 
 
@@ -64,8 +89,8 @@
 def kernel(
     nx, ny, nz,
     panel_hbm, trailing_hbm,
-    pt_ref, wall_ref, factors, trail,
-    pt, gx, gy, gz, schur, wpart, wxrecv, wquarter, wyrecv, wall,
+    pt_high, pt_low, wall_ref, factors, trail,
+    pt, trail_high, trail_low, previous, gx, gy, gz, schur, wpart, wxrecv, wquarter, wyrecv, wall,
     local_sem, z_send, z_recv, p_send, p_recv, send_sem, recv_sem,
 ):
     row, col = lax.axis_index("row"), lax.axis_index("col")
@@ -134,39 +159,79 @@
     def partner_copy(offset, i):
         return remote(block(offset), block(offset), p_send.at[i], p_recv.at[i], partner)
 
-    handed = [0]
+    def split_trailing():
+        load.wait()
+        high, low = split(trail[...])
+        trail_high[...] = high
+        trail_low[...] = low
+
+    handed = [0, 2, -2, 1, -1, 3, -3, 4] if nz == 8 else [0] + z_order
+    each = nz // 2
+    deep, wide_half = wpart.shape[-2], wpart.shape[-1]
+
+    def first_row(offset):
+        return pl.multiple_of(lax.rem(z - offset + nz, nz) * (2 * width), 2 * width)
+
+    def wx_copy(c, d):
+        return remote(
+            wpart.at[c, lax.rem(x + d, nx)], wxrecv.at[c, d - 1], send_sem.at[3 + c], recv_sem.at[3 + c], at_x(d)
+        )
+
+    def half_product(c):
+        parts = []
+        if c == 0:
+            for i in range(each):
+                partner_copy(handed[i], i).wait_recv()
+        for i in range(c * each, (c + 1) * each):
+            source = lax.rem(z - handed[i] + nz, nz) * 2
+            high, low = split(pt[pl.ds(source, 2)].reshape(2 * width, rows))
+            pt_high[pl.ds(first_row(handed[i]), 2 * width), :] = high
+            pt_low[pl.ds(first_row(handed[i]), 2 * width), :] = low
+            parts.append((high, low))
+        left = tuple(jnp.concatenate([part[n] for part in parts], axis=0) for n in range(2))
+        product = dot3(left, (trail_high[...], trail_low[...]), 1, 0)
+        for h in range(2):
+            wpart[c, :, :, h] = product[:, h * wide_half : (h + 1) * wide_half].reshape(nx, ny // 2, deep, wide_half)
+        for d in x_order:
+            wx_copy(c, d).start()
+
     if nz == 8:
         for i, d in enumerate((2, -2, 1, -1)):
             launch(own_copy(d, i))
         launch(partner_copy(0, 0))
+        load.wait()
+        high, low = split(trail[...])
+        trail_high[...] = high
+        trail_low[...] = low
         for i, d in enumerate((2, -2)):
             own_copy(d, i).wait_recv()
             launch(half_copy(d // 2, 4 + i))
             launch(pass_copy(d // 2, 6 + i))
             launch(partner_copy(d, 1 + i))
-            handed.append(d)
         for i, d in enumerate((1, -1)):
             own_copy(d, 2 + i).wait_recv()
             launch(partner_copy(d, 3 + i))
-            handed.append(d)
+        half_product(0)
         for i, d in enumerate((1, -1)):
             pass_copy(d, 6 + i).wait_recv()
             launch(partner_copy(3 * d, 5 + i))
-            handed.append(3 * d)
         for i, d in enumerate((1, -1)):
             half_copy(d, 4 + i).wait_recv()
         launch(partner_copy(4, 7))
-        handed.append(4)
     else:
         for i, d in enumerate(z_order):
             launch(own_copy(d, i))
         launch(partner_copy(0, 0))
+        load.wait()
+        high, low = split(trail[...])
+        trail_high[...] = high
+        trail_low[...] = low
+        half_product(0)
         for i, d in enumerate(z_order):
             own_copy(d, i).wait_recv()
             launch(partner_copy(d, 1 + i))
-            handed.append(d)
-    for i, offset in enumerate(handed):
-        partner_copy(offset, i).wait_recv()
+    for i in range(each, 2 * each):
+        partner_copy(handed[i], i).wait_recv()
 
     tiles = 48 // ncol
     per_block = width // 8
@@ -191,49 +256,47 @@
     def gz_copy(device):
         return remote(gz.at[col], gz.at[col], send_sem.at[2], recv_sem.at[2], device)
 
-    def wx_copy(d):
-        return remote(wpart.at[lax.rem(x + d, nx)], wxrecv.at[d - 1], send_sem.at[3], recv_sem.at[3], at_x(d))
-
-    def wy_copy(d):
-        return remote(wquarter.at[lax.rem(y + d, ny)], wyrecv.at[d - 1], send_sem.at[4], recv_sem.at[4], at_y(d))
-
-    def wa_copy(h, d):
-        return remote(wall.at[h, x, y], wall.at[h, x, y], send_sem.at[5 + h], recv_sem.at[5 + h], at_y(d))
-
-    def wb_copy(h, d):
-        return remote(wall.at[h, x], wall.at[h, x], send_sem.at[7 + h], recv_sem.at[7 + h], at_x(d))
-
-    def sum_x():
-        await_bytes(wxrecv, recv_sem.at[3])
-        value = wpart[x]
+    def wy_copy(c, d):
+        peer = lax.rem(y + d, ny)
+        return remote(
+            wquarter.at[c, peer // 2, lax.rem(peer, 2)], wyrecv.at[c, d - 1], send_sem.at[5 + c], recv_sem.at[5 + c], at_y(d)
+        )
+
+    def wall_slot(c):
+        return wall.at[c, x, y // 2, lax.rem(y, 2)]
+
+    def wa_copy(c, d):
+        return remote(wall_slot(c), wall_slot(c), send_sem.at[7 + c], recv_sem.at[7 + c], at_y(d))
+
+    def wb_copy(c, d):
+        return remote(wall.at[c, x], wall.at[c, x], send_sem.at[9 + c], recv_sem.at[9 + c], at_x(d))
+
+    def sum_x(c):
+        await_bytes(wxrecv.at[c], recv_sem.at[3 + c])
+        value = wpart[c, x]
         for d in range(1, nx):
-            value = value + wxrecv[d - 1]
-        wquarter[...] = value
+            value = value + wxrecv[c, d - 1]
+        wquarter[c] = value
         for d in y_order:
-            wy_copy(d).start()
-
-    columns = wpart.shape[-1]
-
-    def sum_y():
-        await_bytes(wyrecv, recv_sem.at[4])
-        value = wquarter[y]
+            wy_copy(c, d).start()
+
+    def sum_y(c):
+        await_bytes(wyrecv.at[c], recv_sem.at[5 + c])
+        value = wquarter[c, y // 2, lax.rem(y, 2)]
         for d in range(1, ny):
-            value = value + wyrecv[d - 1]
-        for h in range(2):
-            wall[h, x, y] = value[:, h * (columns // 2) : (h + 1) * (columns // 2)]
-        for h in range(2):
-            for d in y_order:
-                wa_copy(h, d).start()
-
-    def spread_x(h):
-        await_bytes(wall.at[h, 0, pl.ds(0, ny - 1)], recv_sem.at[5 + h])
+            value = value + wyrecv[c, d - 1]
+        wall[c, x, y // 2, lax.rem(y, 2)] = value
+        for d in y_order:
+            wa_copy(c, d).start()
+
+    def spread_x(c):
+        await_bytes(wyrecv.at[c], recv_sem.at[7 + c])
         for d in x_order:
-            wb_copy(h, d).start()
+            wb_copy(c, d).start()
 
     for d in x_order:
         gx_copy(d).start()
-    load.wait()
-    wpart[...] = dot(whole, trail[...], 1, 0).reshape(wpart.shape)
+    half_product(1)
     await_bytes(gx.at[pl.ds(0, nx - 1)], recv_sem.at[0])
     total = gx[0]
     for i in range(1, nx):
@@ -241,8 +304,7 @@
     gy[y] = total
     for d in y_order:
         gy_copy(d).start()
-    for d in x_order:
-        wx_copy(d).start()
+    sum_x(0)
     await_bytes(gy.at[pl.ds(0, ny - 1)], recv_sem.at[1])
     total = gy[0]
     for i in range(1, ny):
@@ -252,9 +314,10 @@
         gz_copy(at_z(d)).start()
         gz_copy(at_z(d, True)).start()
     gz_copy(partner).start()
-    sum_x()
-    pt_ref[...] = whole
+    sum_y(0)
+    sum_x(1)
     await_bytes(gz.at[pl.ds(0, ncol - 1)], recv_sem.at[2])
+    sum_y(1)
 
     half = B // 2
     packed = gz[...].reshape(3 * half, half)
@@ -268,53 +331,71 @@
         lax.broadcasted_iota(jnp.int32, (NB, half), 0) == lax.broadcasted_iota(jnp.int32, (NB, half), 1)
     ).astype(F32)
 
+    previous[...] = jnp.zeros_like(previous)
+    lane = lax.broadcasted_iota(jnp.int32, (B - 2 * NB, B), 1)
+    nothing = jnp.zeros((NB, half), F32)
+
     def step(k, carry):
+        old = pltpu.roll(previous[...], 3 * half - NB, 1)[:, 0:B]
+        late = dot(old, old, 0, 0)
         top = jnp.concatenate([schur[0:NB, :], identity], axis=1)
         tiles = [[top[8 * t : 8 * t + 8, 128 * w : 128 * w + 128] for w in range(3)] for t in range(NB // 8)]
         lines = eliminate_panel(tiles, NB)
-        wide = jnp.concatenate([lines, jnp.zeros((NB, half), F32)], axis=1)
+        following = jnp.concatenate([schur[NB : 2 * NB, :] - late[NB : 2 * NB, :], nothing], axis=1)
+        rest = schur[2 * NB : B, :] - late[2 * NB : B, :]
+        high, middle, low = split3(lines)
+        left = jnp.concatenate([high, high, middle, high, middle, low], axis=0)[:, 0:half]
+        right = jnp.concatenate([high, middle, high, low, middle, high], axis=0)
+        following = following - mxu(left, right, 0, 0)[NB : 2 * NB, :]
+        schur[0:NB, :] = pltpu.roll(following, 3 * half - NB, 1)[:, 0:B]
+        schur[NB : B - NB, :] = jnp.where(lane < B - NB, pltpu.roll(rest, B - NB, 1), 0.0)
+        previous[...] = lines
+        wide = jnp.concatenate([lines, nothing], axis=1)
         factors[pl.ds(pl.multiple_of(k * NB, NB), NB), :] = pltpu.roll(wide, k * NB, 1)
-        change = dot(lines[:, 0:B], lines, 0, 0)
-        rest = jnp.concatenate([schur[NB:B, :], jnp.zeros((B - NB, half), F32)], axis=1) - change[NB:B, :]
-        schur[0 : B - NB, :] = pltpu.roll(rest, 3 * half - NB, 1)[:, 0:B]
-        for at, stage in ((0, sum_y), (3, lambda: spread_x(0)), (5, lambda: spread_x(1))):
+        for at, stage in ((0, lambda: spread_x(0)), (4, lambda: spread_x(1))):
             pl.when(k == at)(stage)
         return carry
 
     lax.fori_loop(0, steps, step, 0)
 
-    for h in range(2):
-        await_bytes(wall.at[h, pl.ds(0, nx - 1)], recv_sem.at[7 + h])
-        wall_ref[:, h * (columns // 2) : (h + 1) * (columns // 2)] = wall[h].reshape(B, columns // 2)
+    for c in range(2):
+        await_bytes(wxrecv.at[c], recv_sem.at[9 + c])
+        for h in range(2):
+            value = wall[c, :, :, h].reshape(B // 2, wide_half)
+            for j in range(each):
+                offset = handed[c * each + j]
+                wall_ref[pl.ds(first_row(offset), 2 * width), h * wide_half : (h + 1) * wide_half] = value[
+                    2 * width * j : 2 * width * (j + 1)
+                ]
     for copy in gathered:
         copy.wait_send()
     await_bytes(gx.at[pl.ds(0, nx - 1)], send_sem.at[0])
     await_bytes(gy.at[pl.ds(0, ny - 1)], send_sem.at[1])
     await_bytes(gz.at[pl.ds(0, ncol - 1)], send_sem.at[2])
-    await_bytes(wxrecv, send_sem.at[3])
-    await_bytes(wyrecv, send_sem.at[4])
-    for h in range(2):
-        await_bytes(wall.at[h, 0, pl.ds(0, ny - 1)], send_sem.at[5 + h])
-        await_bytes(wall.at[h, pl.ds(0, nx - 1)], send_sem.at[7 + h])
-
-
-def update_kernel(pt, summed, factors, trail, r_hbm, coupling_hbm, updated_hbm, r_out, coupling_out, out, sems):
+    for c in range(2):
+        await_bytes(wxrecv.at[c], send_sem.at[3 + c])
+        await_bytes(wyrecv.at[c], send_sem.at[5 + c])
+        await_bytes(wyrecv.at[c], send_sem.at[7 + c])
+        await_bytes(wxrecv.at[c], send_sem.at[9 + c])
+
+
+def update_kernel(pt_high, pt_low, summed, factors, trail, r_hbm, coupling_hbm, updated_hbm, r_out, coupling_out, out, sems):
     rows = trail.shape[0]
     upper = lax.broadcasted_iota(jnp.int32, (B, B), 0) <= lax.broadcasted_iota(jnp.int32, (B, B), 1)
     r_out[...] = jnp.where(upper, factors[:, 0:B], 0.0)
     stores = [pltpu.make_async_copy(r_out, r_hbm, sems.at[0])]
     stores[0].start()
-    inverse = factors[:, B : 2 * B]
-    coupling = dot(inverse, summed[...], 1, 0)
+    inverse = split(factors[:, B : 2 * B])
+    coupling = dot3(inverse, split(summed[...]), 1, 0)
     coupling_out[...] = coupling
     stores.append(pltpu.make_async_copy(coupling_out, coupling_hbm, sems.at[1]))
     stores[1].start()
-    weights = dot(inverse, coupling, 0, 0)
+    weights = split(dot3(inverse, split(coupling), 0, 0))
     lines = 128
     for i in range(rows // lines):
-        part = pt[:, i * lines : (i + 1) * lines]
+        part = pt_high[:, i * lines : (i + 1) * lines], pt_low[:, i * lines : (i + 1) * lines]
         span = pl.ds(i * lines, lines)
-        out[span, :] = trail[span, :] - dot(part, weights, 0, 0)
+        out[span, :] = trail[span, :] - dot3(part, weights, 0, 0)
         stores.append(pltpu.make_async_copy(out.at[span], updated_hbm.at[span], sems.at[2 + i]))
         stores[-1].start()
     for store in stores:
@@ -331,33 +412,38 @@
         columns = trailing.shape[1]
         tiles = 48 // ncol
         deep = B // nx // ny
+        half = columns // 2
         dma = pltpu.SemaphoreType.DMA
         hops = max(nz, 8)
-        panel_t, summed, factors, trail = pl.pallas_call(
+        *panel_parts, summed, factors, trail = pl.pallas_call(
             functools.partial(kernel, nx, ny, nz),
             out_shape=(
-                jax.ShapeDtypeStruct((B, rows), F32),
+                jax.ShapeDtypeStruct((B, rows), BF16),
+                jax.ShapeDtypeStruct((B, rows), BF16),
                 jax.ShapeDtypeStruct((B, columns), F32),
                 jax.ShapeDtypeStruct((B, 2 * B), F32),
                 jax.ShapeDtypeStruct((rows, columns), F32),
             ),
             in_specs=[pl.BlockSpec(memory_space=pltpu.HBM)] * 2,
-            out_specs=(pl.BlockSpec(memory_space=pltpu.VMEM),) * 4,
+            out_specs=(pl.BlockSpec(memory_space=pltpu.VMEM),) * 5,
             scratch_shapes=[
                 pltpu.VMEM((ncol, width, rows), F32),
+                pltpu.VMEM((rows, columns), BF16),
+                pltpu.VMEM((rows, columns), BF16),
+                pltpu.VMEM((NB, 3 * B // 2), F32),
                 pltpu.VMEM((nx, tiles, 8, B // 2), F32),
                 pltpu.VMEM((ny, tiles, 8, B // 2), F32),
                 pltpu.VMEM((ncol, tiles, 8, B // 2), F32),
                 pltpu.VMEM((B, B), F32),
-                pltpu.VMEM((nx, ny, deep, columns), F32),
-                pltpu.VMEM((nx - 1, ny, deep, columns), F32),
-                pltpu.VMEM((ny, deep, columns), F32),
-                pltpu.VMEM((ny - 1, deep, columns), F32),
-                pltpu.VMEM((2, nx, ny, deep, columns // 2), F32),
+                pltpu.VMEM((2, nx, ny // 2, 2, deep, half), F32),
+                pltpu.VMEM((2, nx - 1, ny // 2, 2, deep, half), F32),
+                pltpu.VMEM((2, ny // 2, 2, deep, half), F32),
+                pltpu.VMEM((2, ny - 1, deep, half), F32),
+                pltpu.VMEM((2, nx, ny // 2, 2, deep, half), F32),
                 dma((2,)),
                 dma((hops,)), dma((hops,)),
                 dma((hops,)), dma((hops,)),
-                dma((9,)), dma((9,)),
+                dma((11,)), dma((11,)),
             ],
             compiler_params=pltpu.CompilerParams(
                 collective_id=0, has_side_effects=True, vmem_limit_bytes=48 * 1024 * 1024
@@ -372,7 +458,7 @@
                 jax.ShapeDtypeStruct((B, columns), F32),
                 jax.ShapeDtypeStruct((rows, columns), F32),
             ),
-            in_specs=[pl.BlockSpec(memory_space=pltpu.VMEM)] * 4,
+            in_specs=[pl.BlockSpec(memory_space=pltpu.VMEM)] * 5,
             out_specs=(pl.BlockSpec(memory_space=pltpu.HBM),) * 3,
             scratch_shapes=[
                 pltpu.VMEM((B, B), F32),
@@ -381,7 +467,7 @@
                 dma((2 + rows // 128,)),
             ],
             compiler_params=pltpu.CompilerParams(vmem_limit_bytes=32 * 1024 * 1024),
-        )(panel_t, summed, factors, trail)
+        )(*panel_parts, summed, factors, trail)
 
     return jax.shard_map(
         shard,

time: 59.7 us -> 56.8 us (0.951)
  Pallas kernels: 58.9 us -> 56 us
    pallas_call x1, Pallas kernels: 55 us -> 53.4 us  [shard(): pl.pallas_call(functools.partial(kernel, nx, ny, nz), out_shape=(jax.Shap...]
    pallas_call x1, Pallas kernels: 3.88 us -> 2.65 us  [shard(): pl.pallas_call(update_kernel, out_shape=(jax.ShapeDtypeStruct((B, B), F32...]
where the time goes in v4:
time: 56.8 us; the launch traced here: 56.7 us
  Pallas kernels  56 us (99%)
  between operations  0.64 us (1%)
    pallas_call x1, Pallas kernels, shard(): pl.pallas_call(functools.partial(kernel, nx, ny, nz), out_shape=(jax.Shap...  53.4 us
    pallas_call x1, Pallas kernels, shard(): pl.pallas_call(update_kernel, out_shape=(jax.ShapeDtypeStruct((B, B), F32...  2.65 us

profile of v4, /device:TPU:1, one launch (start us, length us, event | category | flops | bytes accessed | tf_op | source)
XLA Modules:
  0.0 56.7 jit_solution(16117104980081561742)
XLA Ops:
  0.6 53.4 %shard_map.49 = (bf16[256,1024]{1,0:T(8,128)(2,1)S(1)}, bf16[256,1024]{1,0:T(8,128)(2,1)S(1)}, f32[256,512]{1,0:T(8,128)S(1)}, f32[256,512]{1,0:T(8,128)S(1)}, f32[1024,512]{1,0:T(8,128)S(1)}) custom-call(f32[16,1024]{1,0:T(8,128)} %bitcast.1, f32[1024,512]{1,0:T(8,128)} %trailing_hbm.1), custom_call_target="tpu_custom_call" | custom-call | tf_op jit(solution)/shard_map/pallas_call | solution.py:418
  54.0 2.7 %shard_map.50 = (f32[256,256]{1,0:T(8,128)}, f32[256,512]{1,0:T(8,128)}, f32[1024,512]{1,0:T(8,128)}) custom-call(bf16[256,1024]{1,0:T(8,128)(2,1)S(1)} %get-tuple-element.8.pt_high, bf16[256,1024]{1,0:T(8,128)(2,1)S(1)} %get-tuple-element.9.pt_low, f32[256,512]{1,0:T(8,128)S(1)} %get-tuple-element.10.summed, f32[256,512]{1,0:T(8,128)S(1)} %get-tuple-element.11.factors, ...), custom_call_target="tpu_custom_call" | custom-call | tf_op jit(solution)/shard_map/pallas_call | solution.py:454

commit v5 on v4

--- a/solution.py
+++ b/solution.py
@@ -46,13 +46,13 @@
     )
 
 
-def eliminate_panel(tiles, rows):
+def eliminate_panel(tiles, rows, start):
     sublane = lax.broadcasted_iota(jnp.int32, (8, 128), 0)
     count = rows // 8
     column = {}
     for c in range(rows):
         for t in range(c // 8, count):
-            column[c, t] = jnp.broadcast_to(tiles[t][0][:, c : c + 1], (8, 128))
+            column[c, t] = jnp.broadcast_to(tiles[t][0][:, start + c : start + c + 1], (8, 128))
 
     def spread(tile, s):
         return jnp.broadcast_to(tile[s : s + 1, :], (8, 128))
@@ -305,6 +305,7 @@
     for d in y_order:
         gy_copy(d).start()
     sum_x(0)
+    sum_x(1)
     await_bytes(gy.at[pl.ds(0, ny - 1)], recv_sem.at[1])
     total = gy[0]
     for i in range(1, ny):
@@ -315,9 +316,8 @@
         gz_copy(at_z(d, True)).start()
     gz_copy(partner).start()
     sum_y(0)
-    sum_x(1)
+    sum_y(1)
     await_bytes(gz.at[pl.ds(0, ncol - 1)], recv_sem.at[2])
-    sum_y(1)
 
     half = B // 2
     packed = gz[...].reshape(3 * half, half)
@@ -325,38 +325,44 @@
     schur[0:half, half:B] = packed[half:B]
     schur[half:B, half:B] = packed[B:]
     schur[half:B, 0:half] = jnp.zeros((half, half), F32)
-    steps = B // NB
-
-    identity = (
-        lax.broadcasted_iota(jnp.int32, (NB, half), 0) == lax.broadcasted_iota(jnp.int32, (NB, half), 1)
-    ).astype(F32)
+    schur[:, B:] = jnp.zeros((B, half), F32)
+    def identity(start):
+        line = lax.broadcasted_iota(jnp.int32, (NB, half), 0)
+        return (line + start == lax.broadcasted_iota(jnp.int32, (NB, half), 1)).astype(F32)
 
     previous[...] = jnp.zeros_like(previous)
-    lane = lax.broadcasted_iota(jnp.int32, (B - 2 * NB, B), 1)
     nothing = jnp.zeros((NB, half), F32)
 
-    def step(k, carry):
-        old = pltpu.roll(previous[...], 3 * half - NB, 1)[:, 0:B]
-        late = dot(old, old, 0, 0)
-        top = jnp.concatenate([schur[0:NB, :], identity], axis=1)
+    def step(k, at, old):
+        late = dot(old[:, 0:B], old, 0, 0)
+        top = jnp.concatenate([schur[at : at + NB, 0:B], schur[at : at + NB, B:] + identity(at)], axis=1)
         tiles = [[top[8 * t : 8 * t + 8, 128 * w : 128 * w + 128] for w in range(3)] for t in range(NB // 8)]
-        lines = eliminate_panel(tiles, NB)
-        following = jnp.concatenate([schur[NB : 2 * NB, :] - late[NB : 2 * NB, :], nothing], axis=1)
-        rest = schur[2 * NB : B, :] - late[2 * NB : B, :]
+        lines = eliminate_panel(tiles, NB, at)
+        after = at + NB
+        schur[after + NB : B, :] = schur[after + NB : B, :] - late[after + NB : B, :]
+        following = schur[after : after + NB, :] - late[after : after + NB, :]
         high, middle, low = split3(lines)
-        left = jnp.concatenate([high, high, middle, high, middle, low], axis=0)[:, 0:half]
+        tile = after // half * half
+        left = jnp.concatenate([high, high, middle, high, middle, low], axis=0)[:, tile : tile + half]
         right = jnp.concatenate([high, middle, high, low, middle, high], axis=0)
-        following = following - mxu(left, right, 0, 0)[NB : 2 * NB, :]
-        schur[0:NB, :] = pltpu.roll(following, 3 * half - NB, 1)[:, 0:B]
-        schur[NB : B - NB, :] = jnp.where(lane < B - NB, pltpu.roll(rest, B - NB, 1), 0.0)
-        previous[...] = lines
+        schur[after : after + NB, :] = following - mxu(left, right, 0, 0)[after - tile : after - tile + NB, :]
         wide = jnp.concatenate([lines, nothing], axis=1)
-        factors[pl.ds(pl.multiple_of(k * NB, NB), NB), :] = pltpu.roll(wide, k * NB, 1)
-        for at, stage in ((0, lambda: spread_x(0)), (4, lambda: spread_x(1))):
-            pl.when(k == at)(stage)
+        place = pl.ds(pl.multiple_of(k * half + at, NB), NB)
+        factors[place, :] = pltpu.roll(wide, k * half, 1)
+        return lines
+
+    def four_steps(k, carry):
+        old = previous[...]
+        for at in range(0, half, NB):
+            old = step(k, at, old)
+            if at in (0, 2 * NB):
+                pl.when(k == 0)(functools.partial(spread_x, at // (2 * NB)))
+        previous[...] = jnp.concatenate([old[:, half:], nothing], axis=1)
+        schur[0:half, 0:B] = schur[half:B, half:]
+        schur[0:half, B:] = jnp.zeros((half, half), F32)
         return carry
 
-    lax.fori_loop(0, steps, step, 0)
+    lax.fori_loop(0, 2, four_steps, 0)
 
     for c in range(2):
         await_bytes(wxrecv.at[c], recv_sem.at[9 + c])
@@ -434,7 +440,7 @@
                 pltpu.VMEM((nx, tiles, 8, B // 2), F32),
                 pltpu.VMEM((ny, tiles, 8, B // 2), F32),
                 pltpu.VMEM((ncol, tiles, 8, B // 2), F32),
-                pltpu.VMEM((B, B), F32),
+                pltpu.VMEM((B, 3 * B // 2), F32),
                 pltpu.VMEM((2, nx, ny // 2, 2, deep, half), F32),
                 pltpu.VMEM((2, nx - 1, ny // 2, 2, deep, half), F32),
                 pltpu.VMEM((2, ny // 2, 2, deep, half), F32),

time: 56.8 us -> 55.6 us (0.979)
  Pallas kernels: 56 us -> 54.8 us
    pallas_call x1, Pallas kernels: 53.4 us -> 52.2 us  [shard(): pl.pallas_call(functools.partial(kernel, nx, ny, nz), out_shape=(jax.Shap...]
where the time goes in v5:
time: 55.6 us; the launch traced here: 55.5 us
  Pallas kernels  54.8 us (99%)
  between operations  0.64 us (1%)
    pallas_call x1, Pallas kernels, shard(): pl.pallas_call(functools.partial(kernel, nx, ny, nz), out_shape=(jax.Shap...  52.2 us
    pallas_call x1, Pallas kernels, shard(): pl.pallas_call(update_kernel, out_shape=(jax.ShapeDtypeStruct((B, B), F32...  2.65 us

profile of v5, /device:TPU:1, one launch (start us, length us, event | category | flops | bytes accessed | tf_op | source)
XLA Modules:
  0.0 55.5 jit_solution(3596107749287260361)
XLA Ops:
  0.6 52.2 %shard_map.49 = (bf16[256,1024]{1,0:T(8,128)(2,1)S(1)}, bf16[256,1024]{1,0:T(8,128)(2,1)S(1)}, f32[256,512]{1,0:T(8,128)S(1)}, f32[256,512]{1,0:T(8,128)S(1)}, f32[1024,512]{1,0:T(8,128)S(1)}) custom-call(f32[16,1024]{1,0:T(8,128)} %bitcast.1, f32[1024,512]{1,0:T(8,128)} %trailing_hbm.1), custom_call_target="tpu_custom_call" | custom-call | tf_op jit(solution)/shard_map/pallas_call | solution.py:424
  52.8 2.6 %shard_map.50 = (f32[256,256]{1,0:T(8,128)}, f32[256,512]{1,0:T(8,128)}, f32[1024,512]{1,0:T(8,128)}) custom-call(bf16[256,1024]{1,0:T(8,128)(2,1)S(1)} %get-tuple-element.8.pt_high, bf16[256,1024]{1,0:T(8,128)(2,1)S(1)} %get-tuple-element.9.pt_low, f32[256,512]{1,0:T(8,128)S(1)} %get-tuple-element.10.summed, f32[256,512]{1,0:T(8,128)S(1)} %get-tuple-element.11.factors, ...), custom_call_target="tpu_custom_call" | custom-call | tf_op jit(solution)/shard_map/pallas_call | solution.py:460
